TPU v7x, 32 devices: a whole 2x2x4 slice. The times are simulated.
32 devices in a mesh: dp: 16 (over z, y, core), tensor: 2 (over x).
Axes of the slice: x: 2, y: 2, z: 4, core: 2. Of those that a mesh axis runs over, the one named last changes fastest.
Arguments:
- hidden_in: bfloat16 [4096, 1024], P(('dp', 'tensor')), may hold values from -6 to 6
- out_grad: bfloat16 [4096, 1024], P(('dp', 'tensor')), may hold values from -6 to 6
- span_start: int32 [16, 2], P('dp'), may hold values from 0 to 240, as said below
- span_length: int32 [16, 2], P('dp'), may hold values from 16 to 128
- attn_gain: bfloat16 [1024], P(('dp', 'tensor')), may hold values from 0.099609375 to 1.8984375
- attn_shift: bfloat16 [1024], P(('dp', 'tensor')), may hold values from -3 to 3
- mlp_gain: bfloat16 [1024], P(('dp', 'tensor')), may hold values from 0.099609375 to 1.8984375
- mlp_shift: bfloat16 [1024], P(('dp', 'tensor')), may hold values from -3 to 3
- qkv_weight: bfloat16 [1024, 3, 1024], P('dp', None, 'tensor'), may hold values from -0.1875 to 0.1875
- qkv_bias: bfloat16 [3, 1024], P(None, ('tensor', 'dp')), may hold values from -3 to 3
- dense_weight: bfloat16 [1024, 1024], P(('tensor', 'dp')), may hold values from -1.5 to 1.5
- dense_bias: bfloat16 [1024], P(('dp', 'tensor')), may hold values from -3 to 3
- up_weight: bfloat16 [1024, 4096], P('dp', 'tensor'), may hold values from -0.1875 to 0.1875
- up_bias: bfloat16 [4096], P(('tensor', 'dp')), may hold values from -3 to 3
- down_weight: bfloat16 [4096, 1024], P(('tensor', 'dp')), may hold values from -0.09375 to 0.09375
- down_bias: bfloat16 [1024], P(('dp', 'tensor')), may hold values from -3 to 3
Outputs:
- layer_out: bfloat16 [4096, 1024], P(('dp', 'tensor'))
- input_grad: bfloat16 [4096, 1024], P(('dp', 'tensor'))
- attn_gain_grad: float32 [1024], P(('dp', 'tensor'))
- attn_shift_grad: float32 [1024], P(('dp', 'tensor'))
- mlp_gain_grad: float32 [1024], P(('dp', 'tensor'))
- mlp_shift_grad: float32 [1024], P(('dp', 'tensor'))
- qkv_weight_grad: float32 [1024, 3, 1024], P('dp', None, 'tensor')
- qkv_bias_grad: float32 [3, 1024], P(None, ('tensor', 'dp'))
- dense_weight_grad: float32 [1024, 1024], P(('tensor', 'dp'))
- dense_bias_grad: float32 [1024], P(('dp', 'tensor'))
- up_weight_grad: float32 [1024, 4096], P('dp', 'tensor')
- up_bias_grad: float32 [4096], P(('tensor', 'dp'))
- down_weight_grad: float32 [4096, 1024], P(('tensor', 'dp'))
- down_bias_grad: float32 [1024], P(('dp', 'tensor'))
Inputs may be any that keep to these rules, and one draw needn't show every extreme that they name: `span_start`: span slot k of a sequence lies inside its positions k * 128 to (k + 1) * 128 - 1.
All inputs are finite; a program needn't handle non-finite values.
Results may differ from a plain program's by a relative error of at most 0.011.
Values may be sent and summed in bfloat16 or wider, within the bound.
A program may use at most 128 MiB of HBM per device.

v0:
```python
import jax
import jax.numpy as jnp
from jax import lax
from jax.sharding import PartitionSpec as P

HD = 64
ROT = 16
NORM_EPS = 1e-05
NEG_FILL = -1000000000.0


def layer_norm(rows_in, gain_vec, shift_vec):
    mean_row = jnp.mean(rows_in, axis=-1, keepdims=True)
    centred = rows_in - mean_row
    spread = jnp.mean(centred * centred, axis=-1, keepdims=True)
    return centred * lax.rsqrt(spread + NORM_EPS) * gain_vec + shift_vec


def rotary_tables(length):
    position = jnp.arange(length, dtype=jnp.float32)
    rates = 10000.0 ** (-jnp.arange(ROT // 2, dtype=jnp.float32) * (2.0 / ROT))
    angles = position[:, None] * rates[None, :]
    angles = jnp.concatenate([angles, angles], axis=-1)[:, None, :]
    return (jnp.cos(angles), jnp.sin(angles))


def rotate(field_in, cosine, sines):
    turned = field_in[..., :ROT]
    first_half = turned[..., : ROT // 2]
    second_half = turned[..., ROT // 2 :]
    swapped = jnp.concatenate([-second_half, first_half], axis=-1)
    return jnp.concatenate([turned * cosine + swapped * sines, field_in[..., ROT:]], axis=-1)


def gelu_exact(values_in):
    return jax.nn.gelu(values_in, approximate=False)


def shards(
    hidden_in,
    out_grad,
    span_start,
    span_length,
    attn_gain,
    attn_shift,
    mlp_gain,
    mlp_shift,
    qkv_weight,
    qkv_bias,
    dense_weight,
    dense_bias,
    up_weight,
    up_bias,
    down_weight,
    down_bias,
):
    local_rows = hidden_in.shape[0]
    length = local_rows * lax.axis_size("tensor")
    block_rows = min(512, length)
    block_count = length // block_rows
    score_scale = HD ** (-0.5)
    small_full = (
        lax.all_gather(attn_gain, ("dp", "tensor"), axis=0, tiled=True),
        lax.all_gather(attn_shift, ("dp", "tensor"), axis=0, tiled=True),
        lax.all_gather(mlp_gain, ("dp", "tensor"), axis=0, tiled=True),
        lax.all_gather(mlp_shift, ("dp", "tensor"), axis=0, tiled=True),
        lax.all_gather(dense_bias, ("dp", "tensor"), axis=0, tiled=True),
        lax.all_gather(down_bias, ("dp", "tensor"), axis=0, tiled=True),
    )
    small_vecs = [item.astype(jnp.float32) for item in small_full]
    own_rows = hidden_in.astype(jnp.float32)
    normed_attn = layer_norm(own_rows, small_vecs[0], small_vecs[1]).astype(jnp.bfloat16)
    normed_mlp = layer_norm(own_rows, small_vecs[2], small_vecs[3]).astype(jnp.bfloat16)
    attn_full, mlp_full = (
        lax.all_gather(normed_attn, "tensor", axis=0, tiled=True),
        lax.all_gather(normed_mlp, "tensor", axis=0, tiled=True),
    )
    full_qkv, full_qkv_bias, full_dense, full_up, full_up_bias, full_down = (
        lax.all_gather(qkv_weight, "dp", axis=0, tiled=True),
        lax.all_gather(qkv_bias, "dp", axis=1, tiled=True),
        lax.all_gather(dense_weight, "dp", axis=0, tiled=True),
        lax.all_gather(up_weight, "dp", axis=0, tiled=True),
        lax.all_gather(up_bias, "dp", axis=0, tiled=True),
        lax.all_gather(down_weight, "dp", axis=0, tiled=True),
    )
    model_width = full_qkv.shape[0]
    head_cols = full_qkv.shape[2]
    local_heads = head_cols // HD
    projected = jnp.dot(
        attn_full, full_qkv.reshape(model_width, 3 * head_cols), preferred_element_type=jnp.float32
    )
    projected = projected + full_qkv_bias.reshape(3 * head_cols).astype(jnp.float32)
    projected = projected.reshape(length, 3, local_heads, HD)
    cosine, sines = rotary_tables(length)
    query_rows = rotate(projected[:, 0], cosine, sines).astype(jnp.bfloat16)
    key_rows = rotate(projected[:, 1], cosine, sines).astype(jnp.bfloat16)
    value_rows = projected[:, 2].astype(jnp.bfloat16)
    position = jnp.arange(length, dtype=jnp.int32)
    starts_here = span_start[0]
    lengths_here = span_length[0]
    inside = (position[None, :] >= starts_here[:, None]) & (
        position[None, :] < (starts_here + lengths_here)[:, None]
    )
    marks = (jnp.arange(starts_here.shape[0], dtype=jnp.int32) + 1)[:, None]
    labels = jnp.sum(jnp.where(inside, marks, 0), axis=0)

    def block_scores(first_row, query_block):
        raw_scores = (
            jnp.einsum("qhe,khe->hqk", query_block, key_rows, preferred_element_type=jnp.float32)
            * score_scale
        )
        row_pos = first_row + jnp.arange(block_rows, dtype=jnp.int32)
        allowed = (position[None, :] <= row_pos[:, None]) | (labels[:, None] == labels[None, :]) & (
            labels[:, None] > 0
        )
        return jnp.where(allowed[None], raw_scores, NEG_FILL)

    def attend(first_row):
        scores = block_scores(first_row, query_rows)
        row_top = jnp.max(scores, axis=-1, keepdims=True)
        exponent = jnp.exp(scores - row_top)
        summed = jnp.sum(exponent, axis=-1, keepdims=True)
        prob_low = (exponent / summed).astype(jnp.bfloat16)
        context_block = jnp.einsum(
            "hqk,khe->qhe", prob_low, value_rows, preferred_element_type=jnp.float32
        )
        return (context_block.astype(jnp.bfloat16), (row_top + jnp.log(summed))[..., 0])

    block_starts = jnp.arange(block_count, dtype=jnp.int32) * block_rows
    context_blocks, lse_blocks = lax.map(attend, block_starts)
    context = context_blocks.reshape(length, head_cols)
    attn_part = jnp.dot(context, full_dense, preferred_element_type=jnp.float32)
    attn_mixed = lax.psum_scatter(
        attn_part.astype(jnp.bfloat16), "tensor", scatter_dimension=0, tiled=True
    ).astype(jnp.float32)
    hidden = jnp.dot(mlp_full, full_up, preferred_element_type=jnp.float32) + full_up_bias.astype(
        jnp.float32
    )
    active = gelu_exact(hidden).astype(jnp.bfloat16)
    mlp_part = jnp.dot(active, full_down, preferred_element_type=jnp.float32)
    mixed_rows = attn_mixed + lax.psum_scatter(
        mlp_part.astype(jnp.bfloat16), "tensor", scatter_dimension=0, tiled=True
    ).astype(jnp.float32)
    layer_out = (own_rows + mixed_rows + small_vecs[4] + small_vecs[5]).astype(jnp.bfloat16)
    cot_full = lax.all_gather(out_grad, "tensor", axis=0, tiled=True)
    full_qkv, full_dense, full_up, full_down = (
        lax.all_gather(qkv_weight, "dp", axis=0, tiled=True),
        lax.all_gather(dense_weight, "dp", axis=0, tiled=True),
        lax.all_gather(up_weight, "dp", axis=0, tiled=True),
        lax.all_gather(down_weight, "dp", axis=0, tiled=True),
    )
    down_grad = jnp.einsum("lf,ld->fd", active, cot_full, preferred_element_type=jnp.float32)
    dense_grad = jnp.einsum("le,ld->ed", context, cot_full, preferred_element_type=jnp.float32)
    active_grad = jnp.einsum("ld,fd->lf", cot_full, full_down, preferred_element_type=jnp.float32)
    hidden_grad = jax.vjp(gelu_exact, hidden)[1](active_grad)[0].astype(jnp.bfloat16)
    up_grad = jnp.einsum("ld,lf->df", mlp_full, hidden_grad, preferred_element_type=jnp.float32)
    up_bias_grad = jnp.sum(hidden_grad, axis=0, dtype=jnp.float32)
    mlp_in_grad = jnp.einsum("lf,df->ld", hidden_grad, full_up, preferred_element_type=jnp.float32)
    context_grad = jnp.einsum("ld,ed->le", cot_full, full_dense, preferred_element_type=jnp.float32)
    context_grad = context_grad.astype(jnp.bfloat16).reshape(length, local_heads, HD)

    def attend_back(carried, inputs):
        key_acc, value_acc = carried
        first_row, lse_block = inputs
        scores = block_scores(first_row, query_rows)
        prob_rows = jnp.exp(scores - lse_block[..., None])
        prob_low = prob_rows.astype(jnp.bfloat16)
        value_acc = value_acc + jnp.einsum(
            "hqk,qhe->khe", prob_low, context_grad, preferred_element_type=jnp.float32
        )
        prob_grad = jnp.einsum(
            "qhe,khe->hqk", context_grad, value_rows, preferred_element_type=jnp.float32
        )
        score_grad = prob_rows * (
            prob_grad - jnp.sum(prob_grad * prob_rows, axis=-1, keepdims=True)
        )
        score_grad = score_grad.astype(jnp.bfloat16)
        query_grad = (
            jnp.einsum("hqk,khe->qhe", score_grad, key_rows, preferred_element_type=jnp.float32)
            * score_scale
        )
        key_acc = (
            key_acc
            + jnp.einsum("hqk,qhe->khe", score_grad, query_rows, preferred_element_type=jnp.float32)
            * score_scale
        )
        return ((key_acc, value_acc), query_grad)

    zero_rows = jnp.zeros((length, local_heads, HD), jnp.float32)
    (key_grad, value_grad), query_blocks = lax.scan(
        attend_back, (zero_rows, zero_rows), (block_starts, lse_blocks)
    )
    query_grad = query_blocks.reshape(length, local_heads, HD)

    def turn(field_in):
        return rotate(field_in, cosine, sines)

    turn_back = jax.vjp(turn, zero_rows)[1]
    projected_grad = jnp.stack(
        [turn_back(query_grad)[0], turn_back(key_grad)[0], value_grad], axis=1
    )
    projected_grad = projected_grad.astype(jnp.bfloat16).reshape(length, 3 * head_cols)
    qkv_weight_grad = jnp.einsum(
        "ld,lc->dc", attn_full, projected_grad, preferred_element_type=jnp.float32
    )
    qkv_weight_grad = qkv_weight_grad.reshape(model_width, 3, head_cols)
    qkv_bias_grad = jnp.sum(projected_grad, axis=0, dtype=jnp.float32).reshape(3, head_cols)
    attn_in_grad = jnp.einsum(
        "lc,dc->ld",
        projected_grad,
        full_qkv.reshape(model_width, 3 * head_cols),
        preferred_element_type=jnp.float32,
    )
    reduced = (
        lax.psum_scatter(qkv_weight_grad, "dp", scatter_dimension=0, tiled=True),
        lax.psum_scatter(qkv_bias_grad, "dp", scatter_dimension=1, tiled=True),
        lax.psum_scatter(dense_grad, "dp", scatter_dimension=0, tiled=True),
        lax.psum_scatter(up_grad, "dp", scatter_dimension=0, tiled=True),
        lax.psum_scatter(up_bias_grad, "dp", scatter_dimension=0, tiled=True),
        lax.psum_scatter(down_grad, "dp", scatter_dimension=0, tiled=True),
    )
    attn_local, mlp_local = (
        lax.psum_scatter(
            attn_in_grad.astype(jnp.bfloat16), "tensor", scatter_dimension=0, tiled=True
        ).astype(jnp.float32),
        lax.psum_scatter(
            mlp_in_grad.astype(jnp.bfloat16), "tensor", scatter_dimension=0, tiled=True
        ).astype(jnp.float32),
    )
    pull_attn = jax.vjp(layer_norm, own_rows, small_vecs[0], small_vecs[1])[1]
    pull_mlp = jax.vjp(layer_norm, own_rows, small_vecs[2], small_vecs[3])[1]
    rows_grad_attn, gain_grad_attn, shift_grad_attn = pull_attn(attn_local)
    rows_grad_mlp, gain_grad_mlp, shift_grad_mlp = pull_mlp(mlp_local)
    cot_rows = out_grad.astype(jnp.float32)
    input_grad = (cot_rows + rows_grad_attn + rows_grad_mlp).astype(jnp.bfloat16)
    bias_total = jnp.sum(cot_rows, axis=0)
    small_sums = (
        lax.psum_scatter(gain_grad_attn, ("dp", "tensor"), scatter_dimension=0, tiled=True),
        lax.psum_scatter(shift_grad_attn, ("dp", "tensor"), scatter_dimension=0, tiled=True),
        lax.psum_scatter(gain_grad_mlp, ("dp", "tensor"), scatter_dimension=0, tiled=True),
        lax.psum_scatter(shift_grad_mlp, ("dp", "tensor"), scatter_dimension=0, tiled=True),
        lax.psum_scatter(bias_total, ("dp", "tensor"), scatter_dimension=0, tiled=True),
    )
    return (
        layer_out,
        input_grad,
        small_sums[0],
        small_sums[1],
        small_sums[2],
        small_sums[3],
        reduced[0],
        reduced[1],
        reduced[2],
        small_sums[4],
        reduced[3],
        reduced[4],
        reduced[5],
        small_sums[4],
    )


def solution(mesh):
    in_specs = (
        P(("dp", "tensor"), None),
        P(("dp", "tensor"), None),
        P("dp", None),
        P("dp", None),
        P(("dp", "tensor")),
        P(("dp", "tensor")),
        P(("dp", "tensor")),
        P(("dp", "tensor")),
        P("dp", None, "tensor"),
        P(None, ("tensor", "dp")),
        P(("tensor", "dp"), None),
        P(("dp", "tensor")),
        P("dp", "tensor"),
        P(("tensor", "dp")),
        P(("tensor", "dp"), None),
        P(("dp", "tensor")),
    )
    out_specs = (
        P(("dp", "tensor"), None),
        P(("dp", "tensor"), None),
        P(("dp", "tensor")),
        P(("dp", "tensor")),
        P(("dp", "tensor")),
        P(("dp", "tensor")),
        P("dp", None, "tensor"),
        P(None, ("tensor", "dp")),
        P(("tensor", "dp"), None),
        P(("dp", "tensor")),
        P("dp", "tensor"),
        P(("tensor", "dp")),
        P(("tensor", "dp"), None),
        P(("dp", "tensor")),
    )
    return jax.shard_map(shards, mesh=mesh, in_specs=in_specs, out_specs=out_specs, check_vma=False)
```

profile of v0, /device:TPU:0, one launch (start us, length us, event | category | flops | bytes accessed | tf_op | source)
XLA Modules:
  0.0 704.2 jit_solution(13958768486302023803)
XLA Ops:
  15.1 42.2 %all-reduce.21 = (bf16[1024]{0:T(1024)(128)(2,1)S(1)}, bf16[1024]{0:T(1024)(128)(2,1)S(1)}, bf16[1024]{0:T(1024)(128)(2,1)S(1)}, bf16[1024]{0:T(1024)(128)(2,1)S...) all-reduce(bf16[1024]{0:T(1024)(128)(2,1)S(1)} %dynamic-update-slic, ...), channel_id=1, replica_groups=mesh['dp'=16,'tensor'=2] {'dp','tensor'}, use_global_device_ids=true, to_apply=%add.11 | all-reduce | flops 6144 | bytes 24576
  57.3 21.3 %all-gather = bf16[16,32,3]{1,2,0:T(4,128)(2,1)S(1)} all-gather(bf16[1,32,3]{1,2,0:T(4,128)(2,1)} %bitcast.96), channel_id=1, replica_groups=mesh['dp'=16,'tensor'=2] {'dp'}, dimensions={0}, use_global_device_ids=true | all-gather | bytes 3264 | tf_op jit(solution)/shard_map/all_gather | solution.py:80
  78.7 17.6 %all-gather.1 = bf16[16,1,128]{2,1,0:T(2,128)(2,1)S(1)} all-gather(bf16[1,1,128]{2,1,0:T(2,128)(2,1)} %bitcast.97), channel_id=1, replica_groups=mesh['dp'=16,'tensor'=2] {'dp'}, dimensions={0}, use_global_device_ids=true | all-gather | bytes 4352 | tf_op jit(solution)/shard_map/all_gather | solution.py:83
  101.4 9.2 %all_gather.51 = bf16[256,1024]{1,0:T(8,128)(2,1)S(1)} all-gather(bf16[128,1024]{1,0:T(8,128)(2,1)S(1)} %get-tuple-element.105), channel_id=1, replica_groups=mesh['dp'=16,'tensor'=2] {'tensor'}, dimensions={0}, use_global_device_ids=true | all-gather | bytes 786432 | tf_op jit(solution)/shard_map/all_gather | solution.py:75
  110.6 8.5 %all_gather.63 = bf16[256,1024]{1,0:T(8,128)(2,1)S(1)} all-gather(bf16[128,1024]{1,0:T(8,128)(2,1)S(1)} %copy-done.9), channel_id=1, replica_groups=mesh['dp'=16,'tensor'=2] {'tensor'}, dimensions={0}, use_global_device_ids=true | all-gather | bytes 786432 | tf_op jit(solution)/shard_map/all_gather | solution.py:145
  119.0 7.7 %all_gather.57 = bf16[256,1024]{1,0:T(8,128)(2,1)} all-gather(bf16[128,1024]{1,0:T(8,128)(2,1)S(1)} %get-tuple-element.106), channel_id=1, replica_groups=mesh['dp'=16,'tensor'=2] {'tensor'}, dimensions={0}, use_global_device_ids=true | all-gather | bytes 786432 | tf_op jit(solution)/shard_map/all_gather | solution.py:76
  126.9 1.7 convolution_convert_fusion.4
  129.4 4.7 copy.67
  134.1 4.1 convolution_add_fusion
  138.2 1.9 copy.69
  142.3 1.6 multiply_reduce_fusion
  147.0 3.8 convolution_convert_fusion.2
  151.1 5.0 convolution_add_fusion.1
  156.1 44.1 %all-gather.13.cloned.1.call-done = bf16[2048,1024]{1,0:T(8,128)(2,1)} async-done(((bf16[128,1024]{1,0:T(8,128)(2,1)}), bf16[2048,1024]{1,0:T(8,128)(2,1)}) %all-gather.13.cloned.1.call-update) | async-done | bytes 4194320 | tf_op jit(solution)/shard_map/all_gather | solution.py:84
  200.2 9.0 %convert_reduce_fusion = (f32[2048]{0:T(1024)S(1)}, bf16[256,2048]{1,0:T(8,128)(2,1)S(1)}, f32[256,2048]{1,0:T(8,128)}) fusion(f32[256,2048]{1,0:T(8,128)} %convolution_add_fusion.1, bf16[256,1024]{1,0:T(8,128)(2,1)S(1)} %all_gather.63, bf16[2048,1024]{1,0:T(8,128)(2,1)} %all-gather.13.cloned.1.call-done), kind=kOutput, calls=%fused_computation.4 | convolution fusion | flops 1112537088 | bytes 9969664 | tf_op jit(solution)/shard_map/ld,fd->lf/dot_general | solution.py:154
  210.2 2.1 convolution_convert_fusion.1
  216.0 2.8 multiply_convert_fusion.1
  219.6 2.1 convolution_convert_fusion.3
  221.8 1.8 fusion.58
  223.6 3.7 fusion.36
  227.4 4.5 fusion.60
  233.3 4.5 fusion.59
  239.7 18.3 %reduce-scatter.28.cloned.1.call-done = f32[32,3]{1,0:T(8,128)} async-done(((f32[512,3]{1,0:T(8,128)}), f32[32,3]{1,0:T(8,128)}) %reduce-scatter.28.cloned.1.call-update) | async-done | bytes 400
  259.3 30.2 %all-reduce.19 = f32[2048]{0:T(1024)S(1)} all-reduce(f32[2048]{0:T(1024)S(1)} %get-tuple-element.92), channel_id=15, replica_groups=mesh['dp'=16,'tensor'=2] {'dp'}, use_global_device_ids=true, to_apply=%region_30.31.clone | all-reduce | flops 2048 | bytes 16384
  293.6 13.8 %reduce-scatter.12.cloned.1.call-done = bf16[128,1024]{1,0:T(8,128)(2,1)} async-done(((bf16[256,1024]{1,0:T(8,128)(2,1)}), bf16[128,1024]{1,0:T(8,128)(2,1)}) %reduce-scatter.12.cloned.1.call-update) | async-done | bytes 262160 | tf_op jit(solution)/shard_map/reduce_scatter | solution.py:133
  307.4 16.9 %reduce-scatter.14.cloned.1.call-done = bf16[128,1024]{1,0:T(8,128)(2,1)} async-done(((bf16[256,1024]{1,0:T(8,128)(2,1)}), bf16[128,1024]{1,0:T(8,128)(2,1)}) %reduce-scatter.14.cloned.1.call-update) | async-done | bytes 262160 | tf_op jit(solution)/shard_map/reduce_scatter | solution.py:141
  324.3 2.4 convert_reduce_fusion.5
  326.8 39.8 %all-reduce.20 = (f32[1024]{0:T(1024)S(1)}, f32[1024]{0:T(1024)S(1)}, f32[1024]{0:T(1024)S(1)}, f32[1024]{0:T(1024)S(1)}, f32[1024]{0:T(1024)S(1)}) all-reduce(f32[1024]{0:T(1024)S(1)} %get-tuple-element.76, f32[1024]{0:T(1024)S(1)} %get-tuple-element.80, ...), channel_id=6, replica_groups=mesh['dp'=16,'tensor'=2] {'dp','tensor'}, use_global_device_ids=true, to_apply=%region_15.16.clone | all-reduce | flops 5120 | bytes 40960
  368.9 21.7 %reduce-scatter.22.cloned.1.call-done = f32[32,1024]{1,0:T(8,128)} async-done(((f32[512,1024]{1,0:T(8,128)}), f32[32,1024]{1,0:T(8,128)}) %reduce-scatter.22.cloned.1.call-update) | async-done | bytes 131088 | tf_op jit(solution)/shard_map/reduce_scatter | solution.py:217
  390.7 89.3 %reduce-scatter.20.cloned.1.call-done = f32[64,3,512]{2,0,1:T(8,128)} async-done(((f32[1024,3,512]{2,0,1:T(8,128)}), f32[64,3,512]{2,0,1:T(8,128)}) %reduce-scatter.20.cloned.1.call-update) | async-done | bytes 393232 | tf_op jit(solution)/shard_map/reduce_scatter | solution.py:215
  479.9 108.2 %reduce-scatter.26.cloned.1.call-done = f32[128,1024]{1,0:T(8,128)} async-done(((f32[2048,1024]{1,0:T(8,128)}), f32[128,1024]{1,0:T(8,128)}) %reduce-scatter.26.cloned.1.call-update) | async-done | bytes 524304 | tf_op jit(solution)/shard_map/reduce_scatter | solution.py:220
  588.1 109.0 %reduce-scatter.24.cloned.1.call-done = f32[64,2048]{1,0:T(8,128)} async-done(((f32[1024,2048]{1,0:T(8,128)}), f32[64,2048]{1,0:T(8,128)}) %reduce-scatter.24.cloned.1.call-update) | async-done | bytes 524304 | tf_op jit(solution)/shard_map/reduce_scatter | solution.py:218
  (139 shorter events, 35.8 us)
Async XLA Ops:
  7.2 103.4 %copy-start.9 = (bf16[128,1024]{1,0:T(8,128)(2,1)S(1)}, bf16[128,1024]{1,0:T(8,128)(2,1)}, u32[]{:S(2)}) copy-start(bf16[128,1024]{1,0:T(8,128)(2,1)} %param.17) | copy-start | bytes 786436
  7.2 119.7 %all-gather.9.cloned.1.call-start = ((), (), s32[]{:S(2)}) async-start(), calls=%async_computation.10 | async-start | bytes 1114112 | tf_op jit(solution)/shard_map/all_gather | solution.py:81
  7.9 121.5 %all-gather.7.cloned.1.call-start = ((), (), s32[]{:S(2)}) async-start(), calls=%async_computation.9 | async-start | bytes 3342336 | tf_op jit(solution)/shard_map/all_gather | solution.py:79
  8.7 142.4 %all-gather.11.cloned.1.call-start = ((), (), s32[]{:S(2)}) async-start(), calls=%async_computation.12 | async-start | bytes 4456448 | tf_op jit(solution)/shard_map/all_gather | solution.py:82
  9.4 190.8 %all-gather.13.cloned.1.call-start = ((), (), s32[]{:S(2)}) async-start(), calls=%async_computation.13 | async-start | bytes 4456448 | tf_op jit(solution)/shard_map/all_gather | solution.py:84
  10.0 248.0 %reduce-scatter.28.cloned.1.call-start = ((), (), s32[]{:S(2)}) async-start(), calls=%async_computation.21 | async-start | bytes 278528
  110.6 23.6 %copy-start.5 = (bf16[256,1024]{1,0:T(8,128)(2,1)}, bf16[256,1024]{1,0:T(8,128)(2,1)S(1)}, u32[]{:S(2)}) copy-start(bf16[256,1024]{1,0:T(8,128)(2,1)S(1)} %all_gather.51) | copy-start | bytes 1572868
  140.1 1.2 copy-start.1
  141.3 1.0 copy-start.3
  147.0 143.2 %reduce-scatter.16.cloned.1.call-start = ((), (), s32[]{:S(2)}) async-start(), calls=%async_computation.15 | async-start | bytes 786432 | tf_op jit(solution)/shard_map/reduce_scatter | solution.py:223
  150.9 139.8 %reduce-scatter.18.cloned.1.call-start = ((), (), s32[]{:S(2)}) async-start(), calls=%async_computation.16 | async-start | bytes 786432 | tf_op jit(solution)/shard_map/reduce_scatter | solution.py:226
  200.2 10.0 %copy-start.14 = (bf16[1024,2048]{1,0:T(8,128)(2,1)S(1)}, bf16[1024,2048]{1,0:T(8,128)(2,1)}, u32[]{:S(2)}) copy-start(bf16[1024,2048]{1,0:T(8,128)(2,1)} %all-gather.11.cloned.1.call-done) | copy-start | bytes 12582916
  209.2 1.0 copy-start.7
  212.3 95.1 %reduce-scatter.12.cloned.1.call-start = ((), (), s32[]{:S(2)}) async-start(), calls=%async_computation.11 | async-start | bytes 786432 | tf_op jit(solution)/shard_map/reduce_scatter | solution.py:133
  212.4 2.3 copy-start.2
  214.0 0.7 copy-start.11
  216.0 108.3 %reduce-scatter.14.cloned.1.call-start = ((), (), s32[]{:S(2)}) async-start(), calls=%async_computation.14 | async-start | bytes 786432 | tf_op jit(solution)/shard_map/reduce_scatter | solution.py:141
  216.0 3.5 copy-start.13
  219.6 2.2 copy-start.12
  221.7 1.9 copy-start.6
  221.7 169.0 %reduce-scatter.22.cloned.1.call-start = ((), (), s32[]{:S(2)}) async-start(), calls=%async_computation.18 | async-start | bytes 2228224 | tf_op jit(solution)/shard_map/reduce_scatter | solution.py:217
  223.6 256.4 %reduce-scatter.20.cloned.1.call-start = ((), (), s32[]{:S(2)}) async-start(), calls=%async_computation.17 | async-start | bytes 6684672 | tf_op jit(solution)/shard_map/reduce_scatter | solution.py:215
  227.4 360.8 %reduce-scatter.26.cloned.1.call-start = ((), (), s32[]{:S(2)}) async-start(), calls=%async_computation.20 | async-start | bytes 8912896 | tf_op jit(solution)/shard_map/reduce_scatter | solution.py:220
  231.9 1.0 copy-start.4
  231.9 1.4 copy-start.8
  232.0 465.2 %reduce-scatter.24.cloned.1.call-start = ((), (), s32[]{:S(2)}) async-start(), calls=%async_computation.19 | async-start | bytes 8912896 | tf_op jit(solution)/shard_map/reduce_scatter | solution.py:218
  237.8 0.7 copy-start.15
  237.8 52.8 %copy-start = (bf16[128,1024]{1,0:T(8,128)(2,1)S(1)}, bf16[128,1024]{1,0:T(8,128)(2,1)}, u32[]{:S(2)}) copy-start(bf16[128,1024]{1,0:T(8,128)(2,1)} %param.16) | copy-start | bytes 786436
  237.8 86.5 %copy-start.10 = (bf16[128,1024]{1,0:T(8,128)(2,1)S(1)}, bf16[128,1024]{1,0:T(8,128)(2,1)}, u32[]{:S(2)}) copy-start(bf16[128,1024]{1,0:T(8,128)(2,1)} %param.17) | copy-start | bytes 786436
  366.6 331.0 %copy-start.16 = (f32[32]{0:T(128)}, f32[32]{0:T(128)S(1)}, u32[]{:S(2)}) copy-start(f32[32]{0:T(128)S(1)} %dynamic-slice.4) | copy-start | bytes 388
Sparse Core Ops, SparseCore 0:
  10.2 40.7 all-gather.8
  53.1 44.3 all-gather.6
  99.7 49.3 all-gather.10
  151.1 49.0 all-gather.12
  204.1 53.7 reduce-scatter.27
  260.1 13.5 reduce-scatter.15
  276.0 14.5 reduce-scatter.17
  292.9 14.5 reduce-scatter.11
  309.8 14.5 reduce-scatter.13
  328.5 62.1 reduce-scatter.21
  395.7 84.1 reduce-scatter.19
  484.4 103.6 reduce-scatter.25
  592.8 104.3 reduce-scatter.23
where the time goes:
time: 705 us; the launch traced here: 704 us
  waiting for transfers between devices  425 us (60%)
  blocking collectives  176 us (25%)
  matrix products  48.5 us (7%)
  local copies, waits for them, and re-layouts  24.5 us (3%)
  between operations  15 us (2%)
  other arithmetic  14.6 us (2%)
    unnamed x3, blocking collectives  112 us
    reduce_scatter x1, waiting for transfers between devices, shards(): lax.psum_scatter(up_grad, 'dp', scatter_dimension=0, tiled=True)  109 us
    reduce_scatter x1, waiting for transfers between devices, shards(): lax.psum_scatter(down_grad, 'dp', scatter_dimension=0, tiled=True)  108 us
    reduce_scatter x1, waiting for transfers between devices, shards(): lax.psum_scatter(qkv_weight_grad, 'dp', scatter_dimension=0, tiled=True)  89.3 us
    all_gather x1, waiting for transfers between devices, shards(): lax.all_gather(down_weight, 'dp', axis=0, tiled=True)  44.1 us
    reduce_scatter x1, waiting for transfers between devices, shards(): lax.psum_scatter(dense_grad, 'dp', scatter_dimension=0, tiled=True)  21.7 us
    all_gather x1, blocking collectives, shards(): lax.all_gather(qkv_bias, 'dp', axis=1, tiled=True)  21.3 us
    unnamed x14, waiting for transfers between devices  21 us
  transfers between devices with their start and end apart: 13, of which 9 were waited for; matrix products, arithmetic and copies ran while one was open for 12% of the time, Pallas kernels for 0%

commit v1 on v0

--- a/solution.py
+++ b/solution.py
@@ -7,6 +7,18 @@
 ROT = 16
 NORM_EPS = 1e-05
 NEG_FILL = -1000000000.0
+
+
+def collect(array, axis, dim):
+    ways, here = (lax.axis_size(axis), lax.axis_index(axis))
+    grown, reach = (array, 1)
+    while reach < ways:
+        theirs = lax.ppermute(grown, axis, [(d, d ^ reach) for d in range(ways)])
+        mine_first = jnp.concatenate([grown, theirs], axis=dim)
+        theirs_first = jnp.concatenate([theirs, grown], axis=dim)
+        grown = jnp.where(here & reach == 0, mine_first, theirs_first)
+        reach = 2 * reach
+    return grown
 
 
 def layer_norm(rows_in, gain_vec, shift_vec):
@@ -80,7 +92,7 @@
         lax.all_gather(qkv_bias, "dp", axis=1, tiled=True),
         lax.all_gather(dense_weight, "dp", axis=0, tiled=True),
         lax.all_gather(up_weight, "dp", axis=0, tiled=True),
-        lax.all_gather(up_bias, "dp", axis=0, tiled=True),
+        collect(up_bias, "dp", 0),
         lax.all_gather(down_weight, "dp", axis=0, tiled=True),
     )
     model_width = full_qkv.shape[0]

time: 705 us -> 705 us (level)
  blocking collectives: 176 us -> 159 us
  waiting for transfers between devices: 425 us -> 442 us
    all_gather x1 -> x0, blocking collectives: 17.6 us -> none  [shards(): lax.all_gather(up_bias, 'dp', axis=0, tiled=True)]
    all_gather x1, waiting for transfers between devices: 0.02 us -> 11.3 us  [shards(): lax.all_gather(up_weight, 'dp', axis=0, tiled=True)]
    unnamed x56 -> x58, local copies, waits for them, and re-layouts: 16.8 us -> 16.7 us
  transfers between devices with their start and end apart: 13 -> 17, of which waited for: 9 -> 11; matrix products, arithmetic and copies ran while one was open for 12% -> 12% of each run, Pallas kernels for 0% -> 0%
where the time goes in v1:
time: 705 us; the launch traced here: 704 us
  waiting for transfers between devices  442 us (63%)
  blocking collectives  159 us (23%)
  matrix products  48.5 us (7%)
  local copies, waits for them, and re-layouts  24.4 us (3%)
  between operations  15 us (2%)
  other arithmetic  14.6 us (2%)
    unnamed x3, blocking collectives  112 us
    reduce_scatter x1, waiting for transfers between devices, shards(): lax.psum_scatter(up_grad, 'dp', scatter_dimension=0, tiled=True)  109 us
    reduce_scatter x1, waiting for transfers between devices, shards(): lax.psum_scatter(down_grad, 'dp', scatter_dimension=0, tiled=True)  108 us
    reduce_scatter x1, waiting for transfers between devices, shards(): lax.psum_scatter(qkv_weight_grad, 'dp', scatter_dimension=0, tiled=True)  89.3 us
    all_gather x1, waiting for transfers between devices, shards(): lax.all_gather(down_weight, 'dp', axis=0, tiled=True)  46.1 us
    reduce_scatter x1, waiting for transfers between devices, shards(): lax.psum_scatter(dense_grad, 'dp', scatter_dimension=0, tiled=True)  21.7 us
    all_gather x1, blocking collectives, shards(): lax.all_gather(qkv_bias, 'dp', axis=1, tiled=True)  21.4 us
    unnamed x14, waiting for transfers between devices  20.4 us
  transfers between devices with their start and end apart: 17, of which 11 were waited for; matrix products, arithmetic and copies ran while one was open for 12% of the time, Pallas kernels for 0%

profile of v1, /device:TPU:0, one launch (start us, length us, event | category | flops | bytes accessed | tf_op | source)
XLA Modules:
  0.0 704.5 jit_solution(11102197790374231231)
XLA Ops:
  15.7 42.2 %all-reduce.21 = (bf16[1024]{0:T(1024)(128)(2,1)S(1)}, bf16[1024]{0:T(1024)(128)(2,1)S(1)}, bf16[1024]{0:T(1024)(128)(2,1)S(1)}, bf16[1024]{0:T(1024)(128)(2,1)S...) all-reduce(bf16[1024]{0:T(1024)(128)(2,1)S(1)} %dynamic-update-slic, ...), channel_id=1, replica_groups=mesh['dp'=16,'tensor'=2] {'dp','tensor'}, use_global_device_ids=true, to_apply=%add.11 | all-reduce | flops 6144 | bytes 24576
  58.0 21.4 %all-gather = bf16[16,32,3]{1,2,0:T(4,128)(2,1)S(1)} all-gather(bf16[1,32,3]{1,2,0:T(4,128)(2,1)} %bitcast.93), channel_id=1, replica_groups=mesh['dp'=16,'tensor'=2] {'dp'}, dimensions={0}, use_global_device_ids=true | all-gather | bytes 3264 | tf_op jit(solution)/shard_map/all_gather | solution.py:92
  83.6 9.2 %all_gather.48 = bf16[256,1024]{1,0:T(8,128)(2,1)S(1)} all-gather(bf16[128,1024]{1,0:T(8,128)(2,1)S(1)} %get-tuple-element.105), channel_id=1, replica_groups=mesh['dp'=16,'tensor'=2] {'tensor'}, dimensions={0}, use_global_device_ids=true | all-gather | bytes 786432 | tf_op jit(solution)/shard_map/all_gather | solution.py:87
  93.2 8.4 %all_gather.59 = bf16[256,1024]{1,0:T(8,128)(2,1)S(1)} all-gather(bf16[128,1024]{1,0:T(8,128)(2,1)S(1)} %copy-done.9), channel_id=1, replica_groups=mesh['dp'=16,'tensor'=2] {'tensor'}, dimensions={0}, use_global_device_ids=true | all-gather | bytes 786432 | tf_op jit(solution)/shard_map/all_gather | solution.py:157
  101.7 7.6 %all_gather.54 = bf16[256,1024]{1,0:T(8,128)(2,1)} all-gather(bf16[128,1024]{1,0:T(8,128)(2,1)S(1)} %get-tuple-element.106), channel_id=1, replica_groups=mesh['dp'=16,'tensor'=2] {'tensor'}, dimensions={0}, use_global_device_ids=true | all-gather | bytes 786432 | tf_op jit(solution)/shard_map/all_gather | solution.py:88
  109.5 4.3 collective-permute-done.3
  113.9 1.7 convolution_convert_fusion.4
  116.4 4.7 copy.67
  121.1 4.1 convolution_add_fusion
  125.2 1.9 copy.69
  134.0 3.8 convolution_convert_fusion.2
  138.0 11.3 %all-gather.10.cloned.1.call-done = bf16[1024,2048]{1,0:T(8,128)(2,1)} async-done(((bf16[64,2048]{1,0:T(8,128)(2,1)}), bf16[1024,2048]{1,0:T(8,128)(2,1)}) %all-gather.10.cloned.1.call-update) | async-done | bytes 4194320 | tf_op jit(solution)/shard_map/all_gather | solution.py:94
  149.3 5.0 fusion.59
  154.3 46.1 %all-gather.12.cloned.1.call-done = bf16[2048,1024]{1,0:T(8,128)(2,1)} async-done(((bf16[128,1024]{1,0:T(8,128)(2,1)}), bf16[2048,1024]{1,0:T(8,128)(2,1)}) %all-gather.12.cloned.1.call-update) | async-done | bytes 4194320 | tf_op jit(solution)/shard_map/all_gather | solution.py:96
  200.4 9.1 %convert_reduce_fusion = (f32[2048]{0:T(1024)S(1)}, bf16[256,2048]{1,0:T(8,128)(2,1)S(1)}, f32[256,2048]{1,0:T(8,128)}) fusion(f32[256,2048]{1,0:T(8,128)} %fusion.59, f32[2048]{0:T(1024)S(1)} %fusion.51, bf16[256,1024]{1,0:T(8,128)(2,1)S(1)} %all_gather.59, bf16[2048,1024]{1,0:T(8,128)(2,1)} %all-gather.12.cloned.1.call-done), kind=kOutput, calls=%fused_computation.3 | convolution fusion | flops 1113061376 | bytes 9977856 | tf_op jit(solution)/shard_map/ld,fd->lf/dot_general | solution.py:166
  210.5 2.1 convolution_convert_fusion.1
  216.3 2.8 multiply_convert_fusion.1
  219.8 2.1 convolution_convert_fusion.3
  222.1 1.8 fusion.60
  223.9 3.7 fusion.36
  227.7 4.5 fusion.62
  233.6 4.5 fusion.61
  240.0 18.2 %reduce-scatter.28.cloned.1.call-done = f32[32,3]{1,0:T(8,128)} async-done(((f32[512,3]{1,0:T(8,128)}), f32[32,3]{1,0:T(8,128)}) %reduce-scatter.28.cloned.1.call-update) | async-done | bytes 400
  259.5 30.2 %all-reduce.19 = f32[2048]{0:T(1024)S(1)} all-reduce(f32[2048]{0:T(1024)S(1)} %get-tuple-element.92), channel_id=15, replica_groups=mesh['dp'=16,'tensor'=2] {'dp'}, use_global_device_ids=true, to_apply=%region_30.31.clone | all-reduce | flops 2048 | bytes 16384
  293.8 13.8 %reduce-scatter.12.cloned.1.call-done = bf16[128,1024]{1,0:T(8,128)(2,1)} async-done(((bf16[256,1024]{1,0:T(8,128)(2,1)}), bf16[128,1024]{1,0:T(8,128)(2,1)}) %reduce-scatter.12.cloned.1.call-update) | async-done | bytes 262160 | tf_op jit(solution)/shard_map/reduce_scatter | solution.py:145
  307.6 16.9 %reduce-scatter.14.cloned.1.call-done = bf16[128,1024]{1,0:T(8,128)(2,1)} async-done(((bf16[256,1024]{1,0:T(8,128)(2,1)}), bf16[128,1024]{1,0:T(8,128)(2,1)}) %reduce-scatter.14.cloned.1.call-update) | async-done | bytes 262160 | tf_op jit(solution)/shard_map/reduce_scatter | solution.py:153
  324.5 2.4 convert_reduce_fusion.5
  327.0 39.8 %all-reduce.20 = (f32[1024]{0:T(1024)S(1)}, f32[1024]{0:T(1024)S(1)}, f32[1024]{0:T(1024)S(1)}, f32[1024]{0:T(1024)S(1)}, f32[1024]{0:T(1024)S(1)}) all-reduce(f32[1024]{0:T(1024)S(1)} %get-tuple-element.76, f32[1024]{0:T(1024)S(1)} %get-tuple-element.80, ...), channel_id=6, replica_groups=mesh['dp'=16,'tensor'=2] {'dp','tensor'}, use_global_device_ids=true, to_apply=%region_15.16.clone | all-reduce | flops 5120 | bytes 40960
  369.1 21.7 %reduce-scatter.22.cloned.1.call-done = f32[32,1024]{1,0:T(8,128)} async-done(((f32[512,1024]{1,0:T(8,128)}), f32[32,1024]{1,0:T(8,128)}) %reduce-scatter.22.cloned.1.call-update) | async-done | bytes 131088 | tf_op jit(solution)/shard_map/reduce_scatter | solution.py:229
  390.9 89.3 %reduce-scatter.20.cloned.1.call-done = f32[64,3,512]{2,0,1:T(8,128)} async-done(((f32[1024,3,512]{2,0,1:T(8,128)}), f32[64,3,512]{2,0,1:T(8,128)}) %reduce-scatter.20.cloned.1.call-update) | async-done | bytes 393232 | tf_op jit(solution)/shard_map/reduce_scatter | solution.py:227
  480.1 108.3 %reduce-scatter.26.cloned.1.call-done = f32[128,1024]{1,0:T(8,128)} async-done(((f32[2048,1024]{1,0:T(8,128)}), f32[128,1024]{1,0:T(8,128)}) %reduce-scatter.26.cloned.1.call-update) | async-done | bytes 524304 | tf_op jit(solution)/shard_map/reduce_scatter | solution.py:232
  588.4 109.0 %reduce-scatter.24.cloned.1.call-done = f32[64,2048]{1,0:T(8,128)} async-done(((f32[1024,2048]{1,0:T(8,128)}), f32[64,2048]{1,0:T(8,128)}) %reduce-scatter.24.cloned.1.call-update) | async-done | bytes 524304 | tf_op jit(solution)/shard_map/reduce_scatter | solution.py:230
  (151 shorter events, 37.5 us)
Async XLA Ops:
  7.2 85.9 %copy-start.13 = (bf16[128]{0:T(256)(128)(2,1)S(1)}, bf16[128]{0:T(256)(128)(2,1)}, u32[]{:S(2)}) copy-start(bf16[128]{0:T(256)(128)(2,1)} %param.29) | copy-start | bytes 772
  7.2 86.0 %copy-start.9 = (bf16[128,1024]{1,0:T(8,128)(2,1)S(1)}, bf16[128,1024]{1,0:T(8,128)(2,1)}, u32[]{:S(2)}) copy-start(bf16[128,1024]{1,0:T(8,128)(2,1)} %param.17) | copy-start | bytes 786436
  7.2 106.7 %all-gather.8.cloned.1.call-start = ((), (), s32[]{:S(2)}) async-start(), calls=%async_computation.10 | async-start | bytes 1114112 | tf_op jit(solution)/shard_map/all_gather | solution.py:93
  7.9 108.5 %all-gather.6.cloned.1.call-start = ((), (), s32[]{:S(2)}) async-start(), calls=%async_computation.9 | async-start | bytes 3342336 | tf_op jit(solution)/shard_map/all_gather | solution.py:91
  8.7 140.6 %all-gather.10.cloned.1.call-start = ((), (), s32[]{:S(2)}) async-start(), calls=%async_computation.12 | async-start | bytes 4456448 | tf_op jit(solution)/shard_map/all_gather | solution.py:94
  9.4 191.0 %all-gather.12.cloned.1.call-start = ((), (), s32[]{:S(2)}) async-start(), calls=%async_computation.13 | async-start | bytes 4456448 | tf_op jit(solution)/shard_map/all_gather | solution.py:96
  9.5 83.6 %collective-permute-start = (bf16[128]{0:T(256)(128)(2,1)}, bf16[128]{0:T(256)(128)(2,1)S(1)}, u32[]{:S(2)}, u32[]{:S(2)}) collective-permute-start(bf16[128]{0:T(256)(128)(2,1)} %param.29), channel_id=1, source_target_pairs={{0,2},{2,0},{4,6},{6,4},{8,10},{10,8},{12,14},{14,12},{16,18},{18,... | collective-permute-start | bytes 776 | tf_op jit(solution)/shard_map/ppermute | solution.py:16
  10.0 248.2 %reduce-scatter.28.cloned.1.call-start = ((), (), s32[]{:S(2)}) async-start(), calls=%async_computation.21 | async-start | bytes 278528
  92.8 28.3 %copy-start.4 = (bf16[256,1024]{1,0:T(8,128)(2,1)}, bf16[256,1024]{1,0:T(8,128)(2,1)S(1)}, u32[]{:S(2)}) copy-start(bf16[256,1024]{1,0:T(8,128)(2,1)S(1)} %all_gather.48) | copy-start | bytes 1572868
  93.1 8.5 %collective-permute-start.1 = (bf16[256]{0:T(256)(128)(2,1)S(1)}, bf16[256]{0:T(256)(128)(2,1)S(1)}, u32[]{:S(2)}, u32[]{:S(2)}) collective-permute-start(bf16[256]{0:T(256)(128)(2,1)S(1)} %broadcast_select_fusion), channel_id=1, source_target_pairs={{0,4},{2,6},{4,0},{6,2},{8,12},{10,14},{12,8},{14,10},{16,20},{18,... | collective-permute-start | bytes 1544 | tf_op jit(solution)/shard_map/ppermute | solution.py:16
  101.6 7.7 %collective-permute-start.2 = (bf16[512]{0:T(512)(128)(2,1)S(1)}, bf16[512]{0:T(512)(128)(2,1)S(1)}, u32[]{:S(2)}, u32[]{:S(2)}) collective-permute-start(bf16[512]{0:T(512)(128)(2,1)S(1)} %maximum_select_fusion.2), channel_id=1, source_target_pairs={{0,8},{2,10},{4,12},{6,14},{8,0},{10,2},{12,4},{14,6},{16,24},{18,... | collective-permute-start | bytes 3080 | tf_op jit(solution)/shard_map/ppermute | solution.py:16
  109.3 4.6 collective-permute-start.3
  127.1 1.2 copy-start.1
  134.0 156.4 %reduce-scatter.16.cloned.1.call-start = ((), (), s32[]{:S(2)}) async-start(), calls=%async_computation.15 | async-start | bytes 786432 | tf_op jit(solution)/shard_map/reduce_scatter | solution.py:235
  137.8 153.0 %reduce-scatter.18.cloned.1.call-start = ((), (), s32[]{:S(2)}) async-start(), calls=%async_computation.16 | async-start | bytes 786432 | tf_op jit(solution)/shard_map/reduce_scatter | solution.py:238
  200.4 10.1 %copy-start.15 = (bf16[1024,2048]{1,0:T(8,128)(2,1)S(1)}, bf16[1024,2048]{1,0:T(8,128)(2,1)}, u32[]{:S(2)}) copy-start(bf16[1024,2048]{1,0:T(8,128)(2,1)} %all-gather.10.cloned.1.call-done) | copy-start | bytes 12582916
  209.5 1.0 copy-start.7
  212.6 95.0 %reduce-scatter.12.cloned.1.call-start = ((), (), s32[]{:S(2)}) async-start(), calls=%async_computation.11 | async-start | bytes 786432 | tf_op jit(solution)/shard_map/reduce_scatter | solution.py:145
  212.7 2.3 copy-start.2
  216.3 108.3 %reduce-scatter.14.cloned.1.call-start = ((), (), s32[]{:S(2)}) async-start(), calls=%async_computation.14 | async-start | bytes 786432 | tf_op jit(solution)/shard_map/reduce_scatter | solution.py:153
  216.3 3.5 copy-start.14
  219.8 2.2 copy-start.12
  222.0 1.9 copy-start.5
  222.0 168.9 %reduce-scatter.22.cloned.1.call-start = ((), (), s32[]{:S(2)}) async-start(), calls=%async_computation.18 | async-start | bytes 2228224 | tf_op jit(solution)/shard_map/reduce_scatter | solution.py:229
  223.9 256.3 %reduce-scatter.20.cloned.1.call-start = ((), (), s32[]{:S(2)}) async-start(), calls=%async_computation.17 | async-start | bytes 6684672 | tf_op jit(solution)/shard_map/reduce_scatter | solution.py:227
  227.6 360.8 %reduce-scatter.26.cloned.1.call-start = ((), (), s32[]{:S(2)}) async-start(), calls=%async_computation.20 | async-start | bytes 8912896 | tf_op jit(solution)/shard_map/reduce_scatter | solution.py:232
  232.2 1.0 copy-start.6
  232.2 1.4 copy-start.8
  232.2 465.2 %reduce-scatter.24.cloned.1.call-start = ((), (), s32[]{:S(2)}) async-start(), calls=%async_computation.19 | async-start | bytes 8912896 | tf_op jit(solution)/shard_map/reduce_scatter | solution.py:230
  238.1 52.7 %copy-start = (bf16[128,1024]{1,0:T(8,128)(2,1)S(1)}, bf16[128,1024]{1,0:T(8,128)(2,1)}, u32[]{:S(2)}) copy-start(bf16[128,1024]{1,0:T(8,128)(2,1)} %param.16) | copy-start | bytes 786436
  238.1 86.4 %copy-start.10 = (bf16[128,1024]{1,0:T(8,128)(2,1)S(1)}, bf16[128,1024]{1,0:T(8,128)(2,1)}, u32[]{:S(2)}) copy-start(bf16[128,1024]{1,0:T(8,128)(2,1)} %param.17) | copy-start | bytes 786436
  366.8 331.1 %copy-start.17 = (f32[32]{0:T(128)}, f32[32]{0:T(128)S(1)}, u32[]{:S(2)}) copy-start(f32[32]{0:T(128)S(1)} %dynamic-slice.4) | copy-start | bytes 388
  (3 other events, 2.3 us)
Sparse Core Ops, SparseCore 0:
  10.2 40.7 all-gather.7
  53.2 44.3 all-gather.5
  99.7 49.5 all-gather.9
  151.3 49.0 all-gather.11
  204.4 53.7 reduce-scatter.27
  260.3 13.5 reduce-scatter.15
  276.2 14.5 reduce-scatter.17
  293.1 14.5 reduce-scatter.11
  310.0 14.5 reduce-scatter.13
  328.7 62.1 reduce-scatter.21
  395.9 84.1 reduce-scatter.19
  484.6 103.7 reduce-scatter.25
  593.0 104.3 reduce-scatter.23
